TPU v7x, 32 devices: a whole 2x2x4 slice. The times are simulated.
32 devices in a mesh: grp: 4 (over y, x), sub: 8 (over z, core).
Axes of the slice: x: 2, y: 2, z: 4, core: 2. Of those that a mesh axis runs over, the one named last changes fastest.
Arguments:
- residual: bfloat16 [4, 8, 1024, 2048], P('grp', 'sub'), may hold values from -6 to 6
- inverse_blocks: bfloat16 [4, 8, 1024, 1536], P('grp', 'sub'), may hold values from -0.15625 to 0.15625
- operator_tiles: bfloat16 [4, 8, 8, 8, 128, 128], P('grp', 'sub'), may hold values from -0.1875 to 0.1875
- column_blocks: int32 [4, 8, 8, 8], P('grp', 'sub'), may hold values from 0 to 11
- coarse_basis: bfloat16 [4, 8, 1024, 200], P('grp', 'sub'), may hold values from -6 to 6
- face_rows: int32 [4, 8, 4, 128], P('grp', 'sub'), may hold values from 0 to 1023
Outputs:
- local_fix: bfloat16 [4, 8, 1024, 2048], P('grp', 'sub')
- galerkin: float32 [200, 200], replicated
- coarse_rhs: float32 [200, 2048], P(None, 'sub')
All inputs are finite; a program needn't handle non-finite values.
Results may differ from a plain program's by a relative error of at most 0.0029.
Values may be sent and summed in bfloat16 or wider, within the bound.
A program may use at most 128 MiB of HBM per device.

v0:
```python
import math
import jax
import jax.numpy as jnp
from jax import lax
from jax.sharding import PartitionSpec as P


def passed_along(x, axis, by):
    devices = lax.axis_size(axis)
    pairs = [(i, i + by) for i in range(devices) if 0 <= i + by < devices]
    return lax.ppermute(x, axis, pairs)


def local(residual, inverse_blocks, operator_tiles, column_blocks, coarse_basis, face_rows):
    resid_own = residual[0, 0]
    basis_own = coarse_basis[0, 0]
    rows_here = face_rows[0, 0]
    resid_face = [jnp.take(resid_own, rows_here[face_index], axis=0) for face_index in range(4)]
    basis_face = [jnp.take(basis_own, rows_here[face_index], axis=0) for face_index in range(4)]
    from_grp_low = passed_along((resid_face[0], basis_face[0]), "grp", 1)
    from_grp_high = passed_along((resid_face[1], basis_face[1]), "grp", -1)
    from_sub_low = passed_along((resid_face[2], basis_face[2]), "sub", 1)
    from_sub_high = passed_along((resid_face[3], basis_face[3]), "sub", -1)
    rhs_term = jnp.einsum("rc,rk->ck", basis_own, resid_own, preferred_element_type=jnp.float32)
    resid_ext = jnp.concatenate(
        [resid_own, from_grp_low[0], from_grp_high[0], from_sub_low[0], from_sub_high[0]], axis=0
    )
    basis_ext = jnp.concatenate(
        [basis_own, from_grp_low[1], from_grp_high[1], from_sub_low[1], from_sub_high[1]], axis=0
    )
    correction = jnp.dot(
        inverse_blocks[0, 0], resid_ext, preferred_element_type=jnp.float32
    ).astype(jnp.bfloat16)
    tile_size = operator_tiles.shape[-1]
    coarse_width = basis_own.shape[1]
    blocks = basis_ext.reshape(-1, tile_size, coarse_width)
    picked = jnp.take(blocks, column_blocks[0, 0], axis=0)
    applied = jnp.einsum(
        "bjtu,bjuc->btc", operator_tiles[0, 0], picked, preferred_element_type=jnp.float32
    )
    applied = applied.reshape(-1, coarse_width).astype(jnp.bfloat16)
    galerkin_term = jnp.einsum("rc,rd->cd", basis_own, applied, preferred_element_type=jnp.float32)
    group_count = lax.axis_size("grp")
    sub_count = lax.axis_size("sub")
    scaling = 1.0 / math.sqrt(resid_own.shape[0] * group_count * sub_count)
    galerkin = lax.psum(galerkin_term, ("grp", "sub")) * scaling
    partial_rhs = lax.psum_scatter(rhs_term, "sub", scatter_dimension=1, tiled=True)
    owned = lax.psum(partial_rhs, "grp")
    coarse_rhs = owned * scaling
    return (correction[None, None], galerkin, coarse_rhs)


def solution(mesh):
    return jax.shard_map(
        local,
        mesh=mesh,
        in_specs=(
            P("grp", "sub", None, None),
            P("grp", "sub", None, None),
            P("grp", "sub", None, None, None, None),
            P("grp", "sub", None, None),
            P("grp", "sub", None, None),
            P("grp", "sub", None, None),
        ),
        out_specs=(P("grp", "sub", None, None), P(), P(None, "sub")),
        check_vma=False,
    )
```

profile of v0, /device:TPU:0, one launch (start us, length us, event | category | flops | bytes accessed | tf_op | source)
XLA Modules:
  0.0 243.4 jit_solution(386409287082498284)
XLA Ops:
  9.0 2.0 copy.13
  13.0 4.9 %collective-permute-start.4 = (bf16[128,200]{1,0:T(8,128)(2,1)S(1)}, bf16[128,200]{1,0:T(8,128)(2,1)S(1)}, u32[]{:S(2)}, u32[]{:S(2)}) collective-permute-start(bf16[128,200]{1,0:T(8,128)(2,1)S(1)} %broadcast_select_fusion.7), channel_id=1, source_target_pairs={{0,8},{8,16},{16,24},{1,9},{9,17},{17,25},{2,10},{10,18},{18,26},{... | collective-permute-start | bytes 153608 | tf_op jit(solution)/shard_map/ppermute | solution.py:11
  23.2 2.1 collective-permute-start.6
  35.2 4.0 %gather_fusion = bf16[64,128,200]{2,1,0:T(8,128)(2,1)} fusion(bf16[12,128,200]{2,1,0:T(8,128)(2,1)} %bitcast.70, s32[1024]{0:T(1024)S(1)} %pad_clamp_fusion), kind=kCustom, calls=%fused_computation.8 | custom fusion | bytes 6553856 | tf_op jit(solution)/shard_map/jit(_take)/gather | solution.py:37
  39.1 6.0 %copy.14 = bf16[64,128,200]{1,2,0:T(8,128)(2,1)} copy(bf16[64,128,200]{2,1,0:T(8,128)(2,1)} %gather_fusion) | data formatting | bytes 6553600 | tf_op jit(solution)/shard_map/jit(_take)/gather | solution.py:37
  45.2 3.7 %fusion.16 = bf16[8,25,8,128]{3,2,1,0:T(8,128)(2,1)S(1)} fusion(bf16[1,1,8,8,128,128]{5,4,3,2,1,0:T(8,128)(2,1)} %param.12, bf16[8,8,128,200]{2,3,1,0:T(8,128)(2,1)} %bitcast.75, pred[8,8]{1,0:T(8,128)(4,1)} %compare_and_fusion), kind=kOutput, calls=%fused_computation.18 | convolution fusion | flops 421273600 | bytes 5783616 | tf_op jit(solution)/shard_map/bjtu,bjuc->btc/dot_general | solution.py:38
  49.9 4.4 %fusion.23 = f32[200,2048]{1,0:T(8,128)} fusion(bf16[1,1,1024,200]{2,3,1,0:T(8,128)(2,1)S(1)} %copy-done.1, bf16[1,1,1024,2048]{3,2,1,0:T(8,128)(2,1)} %param.10), kind=kOutput, calls=%fused_computation.26 | convolution fusion | flops 838860800 | bytes 6242304 | tf_op jit(solution)/shard_map/rc,rk->ck/dot_general | solution.py:24
  54.4 5.1 %gather_fusion.1 = bf16[128,2048]{1,0:T(8,128)(2,1)} fusion(bf16[1024,2048]{1,0:T(8,128)(2,1)} %bitcast.66, s32[1024]{0:T(1024)} %copy-done.3), kind=kCustom, calls=%fused_computation.clone | custom fusion | bytes 1049088 | tf_op jit(solution)/shard_map/jit(_take)/gather | solution.py:18
  59.5 2.0 broadcast_select_fusion.3
  61.5 5.3 %collective-permute-start = (bf16[128,2048]{1,0:T(8,128)(2,1)}, bf16[128,2048]{1,0:T(8,128)(2,1)}, u32[]{:S(2)}, u32[]{:S(2)}) collective-permute-start(bf16[128,2048]{1,0:T(8,128)(2,1)} %broadcast_select_fusion.3), channel_id=1, source_target_pairs={{0,8},{8,16},{16,24},{1,9},{9,17},{17,25},{2,10},{10,18},{18,26},{... | collective-permute-start | bytes 1572872 | tf_op jit(solution)/shard_map/ppermute | solution.py:11
  66.8 5.2 %gather_fusion.2 = bf16[128,2048]{1,0:T(8,128)(2,1)} fusion(bf16[1024,2048]{1,0:T(8,128)(2,1)} %bitcast.67, s32[1024]{0:T(1024)} %copy-done.4), kind=kCustom, calls=%fused_computation.2.clone | custom fusion | bytes 1049088 | tf_op jit(solution)/shard_map/jit(_take)/gather | solution.py:18
  72.0 2.0 broadcast_select_fusion.2
  75.4 5.1 %gather_fusion.3 = bf16[128,2048]{1,0:T(8,128)(2,1)} fusion(bf16[1024,2048]{1,0:T(8,128)(2,1)} %bitcast.68, s32[1024]{0:T(1024)} %copy-done.5), kind=kCustom, calls=%fused_computation.3.clone | custom fusion | bytes 1049088 | tf_op jit(solution)/shard_map/jit(_take)/gather | solution.py:18
  80.5 2.0 broadcast_select_fusion.1
  82.5 4.8 %collective-permute-start.2 = (bf16[128,2048]{1,0:T(8,128)(2,1)}, bf16[128,2048]{1,0:T(8,128)(2,1)}, u32[]{:S(2)}, u32[]{:S(2)}) collective-permute-start(bf16[128,2048]{1,0:T(8,128)(2,1)} %broadcast_select_fusion.1), channel_id=1, source_target_pairs={{0,1},{1,2},{2,3},{3,4},{4,5},{5,6},{6,7},{8,9},{9,10},{10,11},{11... | collective-permute-start | bytes 1572872 | tf_op jit(solution)/shard_map/ppermute | solution.py:11
  87.3 5.1 %gather_fusion.4 = bf16[128,2048]{1,0:T(8,128)(2,1)} fusion(bf16[1024,2048]{1,0:T(8,128)(2,1)} %bitcast.69, s32[1024]{0:T(1024)} %copy-done.6), kind=kCustom, calls=%fused_computation.4.clone | custom fusion | bytes 1049088 | tf_op jit(solution)/shard_map/jit(_take)/gather | solution.py:18
  92.4 2.0 broadcast_select_fusion
  95.9 4.7 %constant_dynamic-update-slice_fusion.4 = bf16[1536,2048]{1,0:T(8,128)(2,1)} fusion(bf16[1,1,1024,2048]{3,2,1,0:T(8,128)(2,1)} %param.10), kind=kLoop, calls=%fused_computation.39 | loop fusion | bytes 8388608
  100.6 81.2 %all-reduce.3.cloned.1.call-done = f32[200,200]{0,1:T(8,128)} async-done(((f32[200,200]{0,1:T(8,128)}), f32[200,200]{0,1:T(8,128)}) %all-reduce.3.cloned.1.call-update) | async-done | bytes 160016 | tf_op jit(solution)/shard_map/psum | solution.py:46
  185.4 1.9 constant_dynamic-update-slice_fusion.2
  189.2 1.9 constant_dynamic-update-slice_fusion
  191.2 11.2 %convert_bitcast_fusion = bf16[1,1,1024,2048]{2,3,1,0:T(8,128)(2,1)} fusion(bf16[1536,2048]{1,0:T(8,128)(2,1)} %constant_dynamic-update-slice_fusion, bf16[1,1,1024,1536]{3,2,1,0:T(8,128)(2,1)S(1)} %copy-done), kind=kOutput, calls=%fused_computation.9 | convolution fusion | flops 6444548096 | bytes 13631488 | tf_op jit(solution)/shard_map/dot_general | solution.py:31
  202.4 6.4 %copy.16 = bf16[1,1,1024,2048]{3,2,1,0:T(8,128)(2,1)} copy(bf16[1,1,1024,2048]{2,3,1,0:T(8,128)(2,1)} %convert_bitcast_fusion) | data formatting | bytes 8388608
  208.8 25.5 %all-reduce.5.cloned.1.call-done = f32[200,256]{1,0:T(8,128)} async-done(((f32[200,256]{1,0:T(8,128)}), f32[200,256]{1,0:T(8,128)}) %all-reduce.5.cloned.1.call-update) | async-done | bytes 204816 | tf_op jit(solution)/shard_map/psum | solution.py:48
  (77 shorter events, 29.1 us)
Async XLA Ops:
  8.0 183.2 %copy-start = (bf16[1,1,1024,1536]{3,2,1,0:T(8,128)(2,1)S(1)}, bf16[1,1,1024,1536]{3,2,1,0:T(8,128)(2,1)}, u32[]{:S(2)}) copy-start(bf16[1,1,1024,1536]{3,2,1,0:T(8,128)(2,1)} %param.11) | copy-start | bytes 9437188
  8.0 23.1 %copy-start.2 = (s32[1,1,8,8]{3,2,1,0:T(8,128)S(1)}, s32[1,1,8,8]{3,2,1,0:T(8,128)}, u32[]{:S(2)}) copy-start(s32[1,1,8,8]{3,2,1,0:T(8,128)} %param.13) | copy-start | bytes 772
  8.0 173.8 %all-reduce.3.cloned.1.call-start = ((), (), s32[]{:S(2)}) async-start(), calls=%async_computation.1 | async-start | bytes 409600 | tf_op jit(solution)/shard_map/psum | solution.py:46
  9.0 10.9 %copy-start.11 = (pred[128]{0:T(512)(128)(4,1)}, pred[128]{0:T(512)(128)(4,1)S(1)}, u32[]{:S(2)}) copy-start(pred[128]{0:T(512)(128)(4,1)S(1)} %get-tuple-element.19) | copy-start | bytes 388
  9.0 10.9 %copy-start.13 = (pred[128]{0:T(512)(128)(4,1)}, pred[128]{0:T(512)(128)(4,1)S(1)}, u32[]{:S(2)}) copy-start(pred[128]{0:T(512)(128)(4,1)S(1)} %get-tuple-element.21) | copy-start | bytes 388
  9.0 16.3 %copy-start.9 = (pred[128]{0:T(512)(128)(4,1)}, pred[128]{0:T(512)(128)(4,1)S(1)}, u32[]{:S(2)}) copy-start(pred[128]{0:T(512)(128)(4,1)S(1)} %get-tuple-element.23) | copy-start | bytes 388
  9.0 30.2 %copy-start.7 = (pred[128]{0:T(512)(128)(4,1)}, pred[128]{0:T(512)(128)(4,1)S(1)}, u32[]{:S(2)}) copy-start(pred[128]{0:T(512)(128)(4,1)S(1)} %get-tuple-element.11) | copy-start | bytes 388
  9.0 3.9 %copy-start.3 = (s32[1024]{0:T(1024)}, s32[1024]{0:T(1024)S(1)}, u32[]{:S(2)}) copy-start(s32[1024]{0:T(1024)S(1)} %pad_clamp_fusion.4) | copy-start | bytes 12292
  13.0 18.8 %collective-permute-start.4 = (bf16[128,200]{1,0:T(8,128)(2,1)S(1)}, bf16[128,200]{1,0:T(8,128)(2,1)S(1)}, u32[]{:S(2)}, u32[]{:S(2)}) collective-permute-start(bf16[128,200]{1,0:T(8,128)(2,1)S(1)} %broadcast_select_fusion.7), channel_id=1, source_target_pairs={{0,8},{8,16},{16,24},{1,9},{9,17},{17,25},{2,10},{10,18},{18,26},{... | collective-permute-start | bytes 153608 | tf_op jit(solution)/shard_map/ppermute | solution.py:11
  19.9 12.5 %collective-permute-start.5 = (bf16[128,200]{1,0:T(8,128)(2,1)S(1)}, bf16[128,200]{1,0:T(8,128)(2,1)S(1)}, u32[]{:S(2)}, u32[]{:S(2)}) collective-permute-start(bf16[128,200]{1,0:T(8,128)(2,1)S(1)} %broadcast_select_fusion.6), channel_id=1, source_target_pairs={{8,0},{16,8},{24,16},{9,1},{17,9},{25,17},{10,2},{18,10},{26,18},{... | collective-permute-start | bytes 153608 | tf_op jit(solution)/shard_map/ppermute | solution.py:11
  23.2 9.9 %collective-permute-start.6 = (bf16[128,200]{1,0:T(8,128)(2,1)S(1)}, bf16[128,200]{1,0:T(8,128)(2,1)}, u32[]{:S(2)}, u32[]{:S(2)}) collective-permute-start(bf16[128,200]{1,0:T(8,128)(2,1)S(1)} %broadcast_select_fusion.5), channel_id=1, source_target_pairs={{0,1},{1,2},{2,3},{3,4},{4,5},{5,6},{6,7},{8,9},{9,10},{10,11},{11... | collective-permute-start | bytes 153608 | tf_op jit(solution)/shard_map/ppermute | solution.py:11
  25.3 3.9 %copy-start.6 = (s32[1024]{0:T(1024)}, s32[1024]{0:T(1024)S(1)}, u32[]{:S(2)}) copy-start(s32[1024]{0:T(1024)S(1)} %pad_clamp_fusion.1) | copy-start | bytes 12292
  27.9 6.6 %collective-permute-start.7 = (bf16[128,200]{1,0:T(8,128)(2,1)}, bf16[128,200]{1,0:T(8,128)(2,1)S(1)}, u32[]{:S(2)}, u32[]{:S(2)}) collective-permute-start(bf16[128,200]{1,0:T(8,128)(2,1)} %broadcast_select_fusion.4), channel_id=1, source_target_pairs={{1,0},{2,1},{3,2},{4,3},{5,4},{6,5},{7,6},{9,8},{10,9},{11,10},{12... | collective-permute-start | bytes 153608 | tf_op jit(solution)/shard_map/ppermute | solution.py:11
  45.2 3.7 %copy-start.1 = (bf16[1,1,1024,200]{2,3,1,0:T(8,128)(2,1)S(1)}, bf16[1,1,1024,200]{2,3,1,0:T(8,128)(2,1)}, u32[]{:S(2)}) copy-start(bf16[1,1,1024,200]{2,3,1,0:T(8,128)(2,1)} %param.14) | copy-start | bytes 1228804
  49.9 141.2 %reduce-scatter.2.cloned.1.call-start = ((), (), s32[]{:S(2)}) async-start(), calls=%async_computation.2 | async-start | bytes 1843200 | tf_op jit(solution)/shard_map/reduce_scatter | solution.py:47
  54.3 5.2 %copy-start.14 = (pred[128]{0:T(512)(128)(4,1)S(1)}, pred[128]{0:T(512)(128)(4,1)}, u32[]{:S(2)}) copy-start(pred[128]{0:T(512)(128)(4,1)} %copy-done.13) | copy-start | bytes 388
  54.3 180.0 %all-reduce.5.cloned.1.call-start = ((), (), s32[]{:S(2)}) async-start(), calls=%async_computation.3 | async-start | bytes 409600 | tf_op jit(solution)/shard_map/psum | solution.py:48
  54.4 17.6 %copy-start.12 = (pred[128]{0:T(512)(128)(4,1)S(1)}, pred[128]{0:T(512)(128)(4,1)}, u32[]{:S(2)}) copy-start(pred[128]{0:T(512)(128)(4,1)} %copy-done.11) | copy-start | bytes 388
  61.5 19.0 %copy-start.10 = (pred[128]{0:T(512)(128)(4,1)S(1)}, pred[128]{0:T(512)(128)(4,1)}, u32[]{:S(2)}) copy-start(pred[128]{0:T(512)(128)(4,1)} %copy-done.9) | copy-start | bytes 388
  61.5 122.0 %collective-permute-start = (bf16[128,2048]{1,0:T(8,128)(2,1)}, bf16[128,2048]{1,0:T(8,128)(2,1)}, u32[]{:S(2)}, u32[]{:S(2)}) collective-permute-start(bf16[128,2048]{1,0:T(8,128)(2,1)} %broadcast_select_fusion.3), channel_id=1, source_target_pairs={{0,8},{8,16},{16,24},{1,9},{9,17},{17,25},{2,10},{10,18},{18,26},{... | collective-permute-start | bytes 1572872 | tf_op jit(solution)/shard_map/ppermute | solution.py:11
  74.0 18.4 %copy-start.8 = (pred[128]{0:T(512)(128)(4,1)S(1)}, pred[128]{0:T(512)(128)(4,1)}, u32[]{:S(2)}) copy-start(pred[128]{0:T(512)(128)(4,1)} %copy-done.7) | copy-start | bytes 388
  74.0 111.4 %collective-permute-start.1 = (bf16[128,2048]{1,0:T(8,128)(2,1)}, bf16[128,2048]{1,0:T(8,128)(2,1)}, u32[]{:S(2)}, u32[]{:S(2)}) collective-permute-start(bf16[128,2048]{1,0:T(8,128)(2,1)} %broadcast_select_fusion.2), channel_id=1, source_target_pairs={{8,0},{16,8},{24,16},{9,1},{17,9},{25,17},{10,2},{18,10},{26,18},{... | collective-permute-start | bytes 1572872 | tf_op jit(solution)/shard_map/ppermute | solution.py:11
  82.5 104.8 %collective-permute-start.2 = (bf16[128,2048]{1,0:T(8,128)(2,1)}, bf16[128,2048]{1,0:T(8,128)(2,1)}, u32[]{:S(2)}, u32[]{:S(2)}) collective-permute-start(bf16[128,2048]{1,0:T(8,128)(2,1)} %broadcast_select_fusion.1), channel_id=1, source_target_pairs={{0,1},{1,2},{2,3},{3,4},{4,5},{5,6},{6,7},{8,9},{9,10},{10,11},{11... | collective-permute-start | bytes 1572872 | tf_op jit(solution)/shard_map/ppermute | solution.py:11
  94.4 94.8 %collective-permute-start.3 = (bf16[128,2048]{1,0:T(8,128)(2,1)}, bf16[128,2048]{1,0:T(8,128)(2,1)}, u32[]{:S(2)}, u32[]{:S(2)}) collective-permute-start(bf16[128,2048]{1,0:T(8,128)(2,1)} %broadcast_select_fusion), channel_id=1, source_target_pairs={{1,0},{2,1},{3,2},{4,3},{5,4},{6,5},{7,6},{9,8},{10,9},{11,10},{12... | collective-permute-start | bytes 1572872 | tf_op jit(solution)/shard_map/ppermute | solution.py:11
  (2 other events, 3.8 us)
Sparse Core Ops, SparseCore 0:
  50.0 131.7 all-reduce.2
Sparse Core Ops, SparseCore 1:
  54.4 39.1 reduce-scatter.1
  191.2 43.0 all-reduce.4
where the time goes:
time: 245 us; the launch traced here: 243 us
  waiting for transfers between devices  107 us (44%)
  local copies, waits for them, and re-layouts  64.9 us (26%)
  starting transfers between devices  22.6 us (9%)
  matrix products  20.2 us (8%)
  between operations  15.8 us (6%)
  other arithmetic  13 us (5%)
    psum x1, waiting for transfers between devices, local(): galerkin = lax.psum(galerkin_term, ('grp', 'sub')) * scaling  81.2 us
    psum x1, waiting for transfers between devices, local(): owned = lax.psum(partial_rhs, 'grp')  25.5 us
    unnamed x41, local copies, waits for them, and re-layouts  24.4 us
    ppermute x8, starting transfers between devices, passed_along(): return lax.ppermute(x, axis, pairs)  22.5 us
    gather x4, local copies, waits for them, and re-layouts, local(): jnp.take(resid_own, rows_here[face_index], axis=0)  20.5 us
    dot_general x1, matrix products, local(): jnp.dot(inverse_blocks[0, 0], resid_ext, preferred_element_type=jnp.float32)  11.2 us
    gather x2, local copies, waits for them, and re-layouts, local(): picked = jnp.take(blocks, column_blocks[0, 0], axis=0)  9.99 us
    select_n x4, other arithmetic, local(): jnp.take(resid_own, rows_here[face_index], axis=0)  7.93 us
  transfers between devices with their start and end apart: 11, of which 2 were waited for; matrix products, arithmetic and copies ran while one was open for 31% of the time, Pallas kernels for 0%

commit v1 on v0

--- a/solution.py
+++ b/solution.py
@@ -43,7 +43,7 @@
     group_count = lax.axis_size("grp")
     sub_count = lax.axis_size("sub")
     scaling = 1.0 / math.sqrt(resid_own.shape[0] * group_count * sub_count)
-    galerkin = lax.psum(galerkin_term, ("grp", "sub")) * scaling
+    galerkin = jnp.sum(lax.all_gather(galerkin_term, ("grp", "sub")), axis=0) * scaling
     partial_rhs = lax.psum_scatter(rhs_term, "sub", scatter_dimension=1, tiled=True)
     owned = lax.psum(partial_rhs, "grp")
     coarse_rhs = owned * scaling

time: 245 us -> 173 us (0.71)
  waiting for transfers between devices: 107 us -> 18.6 us
  other arithmetic: 13 us -> 27.8 us
    psum x1 -> x0, waiting for transfers between devices: 81.2 us -> none  [local(): galerkin = lax.psum(galerkin_term, ('grp', 'sub')) * scaling]
    psum x1, waiting for transfers between devices: 25.5 us -> 0.01 us  [local(): owned = lax.psum(partial_rhs, 'grp')]
    all_gather x0 -> x1, waiting for transfers between devices: none -> 17.3 us  [local(): lax.all_gather(galerkin_term, ('grp', 'sub'))]
    select_n x4, other arithmetic: 0.97 us -> 6.2 us  [local(): jnp.take(basis_own, rows_here[face_index], axis=0)]
    gather x4, other arithmetic: 0.02 us -> 4.31 us
    unnamed x41 -> x24, local copies, waits for them, and re-layouts: 24.4 us -> 20.5 us
    reduce_sum x0 -> x1, other arithmetic: none -> 3.31 us  [local(): jnp.sum(lax.all_gather(galerkin_term, ('grp', 'sub')), axis=0) * scaling]
    gather x4, local copies, waits for them, and re-layouts: 7.46 us -> 10.4 us  [local(): jnp.take(basis_own, rows_here[face_index], axis=0)]
  transfers between devices with their start and end apart: 11 -> 11, of which waited for: 2 -> 2; matrix products, arithmetic and copies ran while one was open for 31% -> 61% of each run, Pallas kernels for 0% -> 0%
where the time goes in v1:
time: 173 us; the launch traced here: 171 us
  local copies, waits for them, and re-layouts  66.1 us (38%)
  other arithmetic  27.8 us (16%)
  starting transfers between devices  23.1 us (13%)
  matrix products  19.8 us (11%)
  waiting for transfers between devices  18.6 us (11%)
  between operations  15.7 us (9%)
    ppermute x8, starting transfers between devices, passed_along(): return lax.ppermute(x, axis, pairs)  23 us
    gather x4, local copies, waits for them, and re-layouts, local(): jnp.take(resid_own, rows_here[face_index], axis=0)  20.6 us
    unnamed x24, local copies, waits for them, and re-layouts  20.5 us
    all_gather x1, waiting for transfers between devices, local(): lax.all_gather(galerkin_term, ('grp', 'sub'))  17.3 us
    gather x4, local copies, waits for them, and re-layouts, local(): jnp.take(basis_own, rows_here[face_index], axis=0)  10.4 us
    gather x2, local copies, waits for them, and re-layouts, local(): picked = jnp.take(blocks, column_blocks[0, 0], axis=0)  10.1 us
    dot_general x1, matrix products, local(): jnp.dot(inverse_blocks[0, 0], resid_ext, preferred_element_type=jnp.float32)  8.69 us
    select_n x4, other arithmetic, local(): jnp.take(resid_own, rows_here[face_index], axis=0)  7.14 us
  transfers between devices with their start and end apart: 11, of which 2 were waited for; matrix products, arithmetic and copies ran while one was open for 61% of the time, Pallas kernels for 0%

profile of v1, /device:TPU:0, one launch (start us, length us, event | category | flops | bytes accessed | tf_op | source)
XLA Modules:
  0.0 171.1 jit_solution(12750319335559022073)
XLA Ops:
  8.1 4.7 %fusion.23 = f32[200,2048]{1,0:T(8,128)} fusion(bf16[1,1,1024,200]{2,3,1,0:T(8,128)(2,1)} %param.14, bf16[1,1,1024,2048]{3,2,1,0:T(8,128)(2,1)} %param.10), kind=kOutput, calls=%fused_computation.26 | convolution fusion | flops 838860800 | bytes 6242304 | tf_op jit(solution)/shard_map/rc,rk->ck/dot_general | solution.py:24
  15.9 2.6 %gather_fusion.5 = bf16[128,200]{1,0:T(8,128)(2,1)} fusion(bf16[1024,200]{1,0:T(8,128)(2,1)} %bitcast.71, s32[1024]{0:T(1024)} %pad_clamp_fusion.4), kind=kCustom, calls=%fused_computation.1.clone | custom fusion | bytes 102912 | tf_op jit(solution)/shard_map/jit(_take)/gather | solution.py:19
  20.1 5.5 %collective-permute-start.4 = (bf16[128,200]{1,0:T(8,128)(2,1)}, bf16[128,200]{1,0:T(8,128)(2,1)}, u32[]{:S(2)}, u32[]{:S(2)}) collective-permute-start(bf16[128,200]{1,0:T(8,128)(2,1)} %broadcast_select_fusion.7), channel_id=1, source_target_pairs={{0,8},{8,16},{16,24},{1,9},{9,17},{17,25},{2,10},{10,18},{18,26},{... | collective-permute-start | bytes 153608 | tf_op jit(solution)/shard_map/ppermute | solution.py:11
  26.8 2.6 %gather_fusion.6 = bf16[128,200]{1,0:T(8,128)(2,1)} fusion(bf16[1024,200]{1,0:T(8,128)(2,1)} %bitcast.72, s32[1024]{0:T(1024)} %pad_clamp_fusion.3), kind=kCustom, calls=%fused_computation.5.clone | custom fusion | bytes 102912 | tf_op jit(solution)/shard_map/jit(_take)/gather | solution.py:19
  33.5 2.6 %gather_fusion.7 = bf16[128,200]{1,0:T(8,128)(2,1)} fusion(bf16[1024,200]{1,0:T(8,128)(2,1)} %bitcast.73, s32[1024]{0:T(1024)} %pad_clamp_fusion.2), kind=kCustom, calls=%fused_computation.6.clone | custom fusion | bytes 102912 | tf_op jit(solution)/shard_map/jit(_take)/gather | solution.py:19
  37.6 2.1 %collective-permute-start.6 = (bf16[128,200]{1,0:T(8,128)(2,1)}, bf16[128,200]{1,0:T(8,128)(2,1)}, u32[]{:S(2)}, u32[]{:S(2)}) collective-permute-start(bf16[128,200]{1,0:T(8,128)(2,1)} %broadcast_select_fusion.5), channel_id=1, source_target_pairs={{0,1},{1,2},{2,3},{3,4},{4,5},{5,6},{6,7},{8,9},{9,10},{10,11},{11... | collective-permute-start | bytes 153608 | tf_op jit(solution)/shard_map/ppermute | solution.py:11
  40.9 2.6 %gather_fusion.8 = bf16[128,200]{1,0:T(8,128)(2,1)} fusion(bf16[1024,200]{1,0:T(8,128)(2,1)} %bitcast.74, s32[1024]{0:T(1024)} %pad_clamp_fusion.1), kind=kCustom, calls=%fused_computation.7.clone | custom fusion | bytes 102912 | tf_op jit(solution)/shard_map/jit(_take)/gather | solution.py:19
  59.1 4.1 %gather_fusion = bf16[64,128,200]{2,1,0:T(8,128)(2,1)} fusion(bf16[12,128,200]{2,1,0:T(8,128)(2,1)} %bitcast.10, s32[1024]{0:T(1024)} %pad_clamp_fusion), kind=kCustom, calls=%fused_computation.8 | custom fusion | bytes 6553856 | tf_op jit(solution)/shard_map/jit(_take)/gather | solution.py:37
  63.2 6.1 %copy.17 = bf16[64,128,200]{1,2,0:T(8,128)(2,1)} copy(bf16[64,128,200]{2,1,0:T(8,128)(2,1)} %gather_fusion) | data formatting | bytes 6553600 | tf_op jit(solution)/shard_map/jit(_take)/gather | solution.py:37
  69.3 4.4 %fusion.16 = bf16[8,25,8,128]{3,2,1,0:T(8,128)(2,1)} fusion(bf16[1,1,8,8,128,128]{5,4,3,2,1,0:T(8,128)(2,1)} %param.12, bf16[8,8,128,200]{2,3,1,0:T(8,128)(2,1)} %bitcast.76, pred[8,8]{1,0:T(8,128)(4,1)} %compare_and_fusion), kind=kOutput, calls=%fused_computation.18 | convolution fusion | flops 421273600 | bytes 5783616 | tf_op jit(solution)/shard_map/bjtu,bjuc->btc/dot_general | solution.py:38
  73.7 2.0 %convolution_bitcast_fusion = f32[200,200]{0,1:T(8,128)} fusion(bf16[8,25,8,128]{3,2,1,0:T(8,128)(2,1)} %fusion.16, bf16[1,1,1024,200]{2,3,1,0:T(8,128)(2,1)S(1)} %copy-done.1), kind=kOutput, calls=%fused_computation.19 | convolution fusion | flops 81920000 | bytes 979200 | tf_op jit(solution)/shard_map/rc,rd->cd/dot_general | solution.py:42
  77.5 5.1 %gather_fusion.1 = bf16[128,2048]{1,0:T(8,128)(2,1)} fusion(bf16[1024,2048]{1,0:T(8,128)(2,1)} %bitcast.67, s32[1024]{0:T(1024)} %pad_clamp_fusion.4), kind=kCustom, calls=%fused_computation.clone | custom fusion | bytes 1049088 | tf_op jit(solution)/shard_map/jit(_take)/gather | solution.py:18
  84.5 5.3 %collective-permute-start = (bf16[128,2048]{1,0:T(8,128)(2,1)}, bf16[128,2048]{1,0:T(8,128)(2,1)}, u32[]{:S(2)}, u32[]{:S(2)}) collective-permute-start(bf16[128,2048]{1,0:T(8,128)(2,1)} %broadcast_select_fusion.3), channel_id=1, source_target_pairs={{0,8},{8,16},{16,24},{1,9},{9,17},{17,25},{2,10},{10,18},{18,26},{... | collective-permute-start | bytes 1572872 | tf_op jit(solution)/shard_map/ppermute | solution.py:11
  89.9 5.2 %gather_fusion.2 = bf16[128,2048]{1,0:T(8,128)(2,1)} fusion(bf16[1024,2048]{1,0:T(8,128)(2,1)} %bitcast.68, s32[1024]{0:T(1024)} %pad_clamp_fusion.3), kind=kCustom, calls=%fused_computation.2.clone | custom fusion | bytes 1049088 | tf_op jit(solution)/shard_map/jit(_take)/gather | solution.py:18
  95.1 2.0 %broadcast_select_fusion.2 = bf16[128,2048]{1,0:T(8,128)(2,1)} fusion(bf16[128,2048]{1,0:T(8,128)(2,1)} %gather_fusion.2, pred[128]{0:T(512)(128)(4,1)S(1)} %copy-done.4), kind=kLoop, calls=%fused_computation.22 | loop fusion | flops 262144 | bytes 1048704 | tf_op jit(solution)/shard_map/jit(_take)/select_n | solution.py:18
  98.5 5.2 %gather_fusion.3 = bf16[128,2048]{1,0:T(8,128)(2,1)} fusion(bf16[1024,2048]{1,0:T(8,128)(2,1)} %bitcast.69, s32[1024]{0:T(1024)} %pad_clamp_fusion.2), kind=kCustom, calls=%fused_computation.3.clone | custom fusion | bytes 1049088 | tf_op jit(solution)/shard_map/jit(_take)/gather | solution.py:18
  103.7 2.0 %broadcast_select_fusion.1 = bf16[128,2048]{1,0:T(8,128)(2,1)} fusion(bf16[128,2048]{1,0:T(8,128)(2,1)} %gather_fusion.3, pred[128]{0:T(512)(128)(4,1)S(1)} %copy-done.3), kind=kLoop, calls=%fused_computation.21 | loop fusion | flops 262144 | bytes 1048704 | tf_op jit(solution)/shard_map/jit(_take)/select_n | solution.py:18
  105.8 4.7 %collective-permute-start.2 = (bf16[128,2048]{1,0:T(8,128)(2,1)}, bf16[128,2048]{1,0:T(8,128)(2,1)}, u32[]{:S(2)}, u32[]{:S(2)}) collective-permute-start(bf16[128,2048]{1,0:T(8,128)(2,1)} %broadcast_select_fusion.1), channel_id=1, source_target_pairs={{0,1},{1,2},{2,3},{3,4},{4,5},{5,6},{6,7},{8,9},{9,10},{10,11},{11... | collective-permute-start | bytes 1572872 | tf_op jit(solution)/shard_map/ppermute | solution.py:11
  110.4 5.1 %gather_fusion.4 = bf16[128,2048]{1,0:T(8,128)(2,1)} fusion(bf16[1024,2048]{1,0:T(8,128)(2,1)} %bitcast.70, s32[1024]{0:T(1024)} %pad_clamp_fusion.1), kind=kCustom, calls=%fused_computation.4.clone | custom fusion | bytes 1049088 | tf_op jit(solution)/shard_map/jit(_take)/gather | solution.py:18
  118.1 2.5 %constant_dynamic-update-slice_fusion.4 = bf16[1536,2048]{1,0:T(8,128)(2,1)S(1)} fusion(bf16[1,1,1024,2048]{3,2,1,0:T(8,128)(2,1)} %param.10), kind=kLoop, calls=%fused_computation.39 | loop fusion | bytes 8388608
  125.3 8.7 %convert_bitcast_fusion = bf16[1,1,1024,2048]{2,3,1,0:T(8,128)(2,1)} fusion(bf16[1536,2048]{1,0:T(8,128)(2,1)S(1)} %constant_dynamic-update-slice_fusion, bf16[1,1,1024,1536]{3,2,1,0:T(8,128)(2,1)S(1)} %copy-done), kind=kOutput, calls=%fused_computation.9 | convolution fusion | flops 6444548096 | bytes 13631488 | tf_op jit(solution)/shard_map/dot_general | solution.py:31
  134.0 6.5 %copy.21 = bf16[1,1,1024,2048]{3,2,1,0:T(8,128)(2,1)} copy(bf16[1,1,1024,2048]{2,3,1,0:T(8,128)(2,1)} %convert_bitcast_fusion) | data formatting | bytes 8388608
  142.1 17.3 %all-gather.3.cloned.1.call-done = f32[6400,200]{1,0:T(8,128)} async-done(((f32[200,200]{1,0:T(8,128)}), f32[6400,200]{1,0:T(8,128)}) %all-gather.3.cloned.1.call-update) | async-done | bytes 5120016 | tf_op jit(solution)/shard_map/all_gather | solution.py:46
  159.4 3.3 %reduce_sum.9 = f32[200,200]{1,0:T(8,128)S(1)} reduce(f32[32,200,200]{2,1,0:T(8,128)} %bitcast.75, f32[]{:T(128)} %constant.30.clone.1), dimensions={0}, to_apply=%region_0.3 | reduce | flops 1240000 | bytes 5280004 | tf_op jit(solution)/shard_map/reduce_sum | solution.py:46
  (62 shorter events, 43.3 us)
Async XLA Ops:
  8.0 117.3 %copy-start = (bf16[1,1,1024,1536]{3,2,1,0:T(8,128)(2,1)S(1)}, bf16[1,1,1024,1536]{3,2,1,0:T(8,128)(2,1)}, u32[]{:S(2)}) copy-start(bf16[1,1,1024,1536]{3,2,1,0:T(8,128)(2,1)} %param.11) | copy-start | bytes 9437188
  8.0 4.8 %copy-start.1 = (bf16[1,1,1024,200]{2,3,1,0:T(8,128)(2,1)S(1)}, bf16[1,1,1024,200]{2,3,1,0:T(8,128)(2,1)}, u32[]{:S(2)}) copy-start(bf16[1,1,1024,200]{2,3,1,0:T(8,128)(2,1)} %param.14) | copy-start | bytes 1228804
  8.0 65.6 %reduce-scatter.2.cloned.1.call-start = ((), (), s32[]{:S(2)}) async-start(), calls=%async_computation.1 | async-start | bytes 1843200 | tf_op jit(solution)/shard_map/reduce_scatter | solution.py:47
  12.8 127.7 %all-reduce.2.cloned.1.call-start = ((), (), s32[]{:S(2)}) async-start(), calls=%async_computation.2 | async-start | bytes 409600 | tf_op jit(solution)/shard_map/psum | solution.py:48
  20.1 33.2 %collective-permute-start.4 = (bf16[128,200]{1,0:T(8,128)(2,1)}, bf16[128,200]{1,0:T(8,128)(2,1)}, u32[]{:S(2)}, u32[]{:S(2)}) collective-permute-start(bf16[128,200]{1,0:T(8,128)(2,1)} %broadcast_select_fusion.7), channel_id=1, source_target_pairs={{0,8},{8,16},{16,24},{1,9},{9,17},{17,25},{2,10},{10,18},{18,26},{... | collective-permute-start | bytes 153608 | tf_op jit(solution)/shard_map/ppermute | solution.py:11
  31.0 23.7 %collective-permute-start.5 = (bf16[128,200]{1,0:T(8,128)(2,1)}, bf16[128,200]{1,0:T(8,128)(2,1)}, u32[]{:S(2)}, u32[]{:S(2)}) collective-permute-start(bf16[128,200]{1,0:T(8,128)(2,1)} %broadcast_select_fusion.6), channel_id=1, source_target_pairs={{8,0},{16,8},{24,16},{9,1},{17,9},{25,17},{10,2},{18,10},{26,18},{... | collective-permute-start | bytes 153608 | tf_op jit(solution)/shard_map/ppermute | solution.py:11
  37.6 18.6 %collective-permute-start.6 = (bf16[128,200]{1,0:T(8,128)(2,1)}, bf16[128,200]{1,0:T(8,128)(2,1)}, u32[]{:S(2)}, u32[]{:S(2)}) collective-permute-start(bf16[128,200]{1,0:T(8,128)(2,1)} %broadcast_select_fusion.5), channel_id=1, source_target_pairs={{0,1},{1,2},{2,3},{3,4},{4,5},{5,6},{6,7},{8,9},{9,10},{10,11},{11... | collective-permute-start | bytes 153608 | tf_op jit(solution)/shard_map/ppermute | solution.py:11
  45.1 12.6 %collective-permute-start.7 = (bf16[128,200]{1,0:T(8,128)(2,1)}, bf16[128,200]{1,0:T(8,128)(2,1)}, u32[]{:S(2)}, u32[]{:S(2)}) collective-permute-start(bf16[128,200]{1,0:T(8,128)(2,1)} %broadcast_select_fusion.4), channel_id=1, source_target_pairs={{1,0},{2,1},{3,2},{4,3},{5,4},{6,5},{7,6},{9,8},{10,9},{11,10},{12... | collective-permute-start | bytes 153608 | tf_op jit(solution)/shard_map/ppermute | solution.py:11
  73.7 85.7 %all-gather.3.cloned.1.call-start = ((), (), s32[]{:S(2)}) async-start(), calls=%async_computation.3 | async-start | bytes 6758400 | tf_op jit(solution)/shard_map/all_gather | solution.py:46
  75.7 6.9 %copy-start.5 = (pred[128]{0:T(512)(128)(4,1)S(1)}, pred[128]{0:T(512)(128)(4,1)}, u32[]{:S(2)}) copy-start(pred[128]{0:T(512)(128)(4,1)} %get-tuple-element.24) | copy-start | bytes 388
  77.5 17.6 %copy-start.4 = (pred[128]{0:T(512)(128)(4,1)S(1)}, pred[128]{0:T(512)(128)(4,1)}, u32[]{:S(2)}) copy-start(pred[128]{0:T(512)(128)(4,1)} %get-tuple-element.22) | copy-start | bytes 388
  84.5 19.2 %copy-start.3 = (pred[128]{0:T(512)(128)(4,1)S(1)}, pred[128]{0:T(512)(128)(4,1)}, u32[]{:S(2)}) copy-start(pred[128]{0:T(512)(128)(4,1)} %get-tuple-element.26) | copy-start | bytes 388
  84.5 36.1 %collective-permute-start = (bf16[128,2048]{1,0:T(8,128)(2,1)}, bf16[128,2048]{1,0:T(8,128)(2,1)}, u32[]{:S(2)}, u32[]{:S(2)}) collective-permute-start(bf16[128,2048]{1,0:T(8,128)(2,1)} %broadcast_select_fusion.3), channel_id=1, source_target_pairs={{0,8},{8,16},{16,24},{1,9},{9,17},{17,25},{2,10},{10,18},{18,26},{... | collective-permute-start | bytes 1572872 | tf_op jit(solution)/shard_map/ppermute | solution.py:11
  97.1 18.4 %copy-start.2 = (pred[128]{0:T(512)(128)(4,1)S(1)}, pred[128]{0:T(512)(128)(4,1)}, u32[]{:S(2)}) copy-start(pred[128]{0:T(512)(128)(4,1)} %get-tuple-element.14) | copy-start | bytes 388
  97.1 25.9 %collective-permute-start.1 = (bf16[128,2048]{1,0:T(8,128)(2,1)}, bf16[128,2048]{1,0:T(8,128)(2,1)}, u32[]{:S(2)}, u32[]{:S(2)}) collective-permute-start(bf16[128,2048]{1,0:T(8,128)(2,1)} %broadcast_select_fusion.2), channel_id=1, source_target_pairs={{8,0},{16,8},{24,16},{9,1},{17,9},{25,17},{10,2},{18,10},{26,18},{... | collective-permute-start | bytes 1572872 | tf_op jit(solution)/shard_map/ppermute | solution.py:11
  105.8 18.4 %collective-permute-start.2 = (bf16[128,2048]{1,0:T(8,128)(2,1)}, bf16[128,2048]{1,0:T(8,128)(2,1)}, u32[]{:S(2)}, u32[]{:S(2)}) collective-permute-start(bf16[128,2048]{1,0:T(8,128)(2,1)} %broadcast_select_fusion.1), channel_id=1, source_target_pairs={{0,1},{1,2},{2,3},{3,4},{4,5},{5,6},{6,7},{8,9},{9,10},{10,11},{11... | collective-permute-start | bytes 1572872 | tf_op jit(solution)/shard_map/ppermute | solution.py:11
  116.7 8.6 %collective-permute-start.3 = (bf16[128,2048]{1,0:T(8,128)(2,1)S(1)}, bf16[128,2048]{1,0:T(8,128)(2,1)S(1)}, u32[]{:S(2)}, u32[]{:S(2)}) collective-permute-start(bf16[128,2048]{1,0:T(8,128)(2,1)S(1)} %broadcast_select_fusion), channel_id=1, source_target_pairs={{1,0},{2,1},{3,2},{4,3},{5,4},{6,5},{7,6},{9,8},{10,9},{11,10},{12... | collective-permute-start | bytes 1572872 | tf_op jit(solution)/shard_map/ppermute | solution.py:11
Sparse Core Ops, SparseCore 0:
  12.9 37.5 reduce-scatter.1
  73.8 50.4 all-reduce.1
Sparse Core Ops, SparseCore 1:
  77.6 81.7 all-gather.2
